TPU v7x, 32 devices: a whole 2x2x4 slice. The times are simulated.
32 devices in a mesh: point: 8 (over y, x, core), batch: 4 (over z).
Axes of the slice: x: 2, y: 2, z: 4, core: 2. Of those that a mesh axis runs over, the one named last changes fastest.
Arguments:
- activations: bfloat16 [128, 14, 14, 1024], P('batch'), may hold values from -8 to 8
- labels: int32 [128], P('batch'), may hold values from 0 to 999
- t_values: float32 [64], replicated, may hold values from 0 to 1
- point_index: int32 [8], replicated, may hold values from 0 to 63
- w_reduce: bfloat16 [3, 1024, 256], P(None, 'point'), may hold values from -1 to 1
- w_spatial: bfloat16 [3, 2304, 256], P(None, 'point'), may hold values from -0.125 to 0.125
- w_expand: bfloat16 [3, 256, 1024], P(None, 'point'), may hold values from -0.375 to 0.375
- w_classes: bfloat16 [3, 1000, 1024], P(None, None, 'point'), may hold values from -0.1875 to 0.1875
- norm_gain: float32 [3, 1536], replicated, may hold values from 0.5 to 1.5
- norm_bias: float32 [3, 1536], replicated, may hold values from -3 to 3
- class_bias: float32 [3, 1000], replicated, may hold values from -3 to 3
Outputs:
- mean_reduce: float32 [8, 256], P('point')
- var_reduce: float32 [8, 256], P('point')
- mean_spatial: float32 [8, 256], P('point')
- var_spatial: float32 [8, 256], P('point')
- mean_expand: float32 [8, 1024], P('point')
- var_expand: float32 [8, 1024], P('point')
- margin: float32 [8], replicated
All inputs are finite; a program needn't handle non-finite values.
Results may differ from a plain program's by a relative error of at most 0.003.
Values may be sent and summed in bfloat16 or wider, within the bound.
A program may use at most 128 MiB of HBM per device.

v0:
```python
import jax
import jax.numpy as jnp
from jax import lax
from jax.sharding import PartitionSpec as P

EPSILON = 1e-05


def curve_coefficients(t_values, point_index):
    table_size = t_values.shape[0]
    matches = point_index[:, None] == jnp.arange(table_size, dtype=jnp.int32)[None, :]
    picked = jnp.sum(jnp.where(matches, t_values[None, :], 0.0), axis=1)
    doubled = 2.0 * picked
    return jnp.stack(
        [
            jnp.maximum(1.0 - doubled, 0.0),
            1.0 - jnp.abs(1.0 - doubled),
            jnp.maximum(doubled - 1.0, 0.0),
        ],
        axis=1,
    )


def blend_all(coefficients, endpoints):
    target_shape = (coefficients.shape[0],) + (1,) * (endpoints.ndim - 1)
    start_part = coefficients[:, 0].reshape(target_shape) * endpoints[0].astype(jnp.float32)[None]
    bend_part = coefficients[:, 1].reshape(target_shape) * endpoints[1].astype(jnp.float32)[None]
    final_part = coefficients[:, 2].reshape(target_shape) * endpoints[2].astype(jnp.float32)[None]
    return start_part + bend_part + final_part


def point_weight(endpoints, own_row, by_columns):
    if by_columns:
        gathered = lax.all_gather(endpoints, "point", axis=2, tiled=True)
    else:
        gathered = lax.all_gather(endpoints, "point", axis=1, tiled=True)
    return blend_all(own_row, gathered)[0].astype(jnp.bfloat16)


def map_product(maps, kernel):
    return lax.dot_general(
        maps, kernel, (((3,), (0,)), ((), ())), preferred_element_type=jnp.float32
    )


def batch_norm(pre_norm, gain_part, bias_part, row_count):
    channel_total, channel_squares = lax.psum(
        (jnp.sum(pre_norm, axis=(0, 1, 2)), jnp.sum(pre_norm * pre_norm, axis=(0, 1, 2))), "batch"
    )
    channel_mean = channel_total / row_count
    channel_var = channel_squares / row_count - channel_mean * channel_mean
    scaled = (pre_norm - channel_mean) * lax.rsqrt(channel_var + EPSILON) * gain_part + bias_part
    return (channel_mean, channel_var, scaled)


def spatial_conv(source, kernel):
    side_len = source.shape[1]
    middle = source.shape[3]
    padded = jnp.pad(source, ((0, 0), (1, 1), (1, 1), (0, 0)))
    widened = jnp.concatenate(
        [
            padded[:, :, 0:side_len, :],
            padded[:, :, 1 : side_len + 1, :],
            padded[:, :, 2 : side_len + 2, :],
        ],
        axis=3,
    )
    summed = map_product(widened[:, 0:side_len], kernel[0 : 3 * middle])
    summed = summed + map_product(widened[:, 1 : side_len + 1], kernel[3 * middle : 6 * middle])
    summed = summed + map_product(widened[:, 2 : side_len + 2], kernel[6 * middle : 9 * middle])
    return summed


def shards(
    activations,
    labels,
    t_values,
    point_index,
    w_reduce,
    w_spatial,
    w_expand,
    w_classes,
    norm_gain,
    norm_bias,
    class_bias,
):
    coefficients = curve_coefficients(t_values, point_index)
    own_row = lax.dynamic_slice_in_dim(coefficients, lax.axis_index("point"), 1, 0)
    reduce_w = point_weight(w_reduce, own_row, False)
    spatial_w = point_weight(w_spatial, own_row, False)
    expand_w = point_weight(w_expand, own_row, False)
    class_w = point_weight(w_classes, own_row, True)
    gain_now = blend_all(own_row, norm_gain)[0]
    bias_now = blend_all(own_row, norm_bias)[0]
    shift_now = blend_all(own_row, class_bias)[0]
    images, side_len, _, channels = activations.shape
    middle = w_reduce.shape[2]
    row_count = float(images * side_len * side_len * lax.axis_size("batch"))
    reduced = map_product(activations, reduce_w)
    mean_one, var_one, normed_one = batch_norm(
        reduced, gain_now[:middle], bias_now[:middle], row_count
    )
    first = jax.nn.relu(normed_one).astype(jnp.bfloat16)
    spatial = spatial_conv(first, spatial_w)
    mean_two, var_two, normed_two = batch_norm(
        spatial, gain_now[middle : 2 * middle], bias_now[middle : 2 * middle], row_count
    )
    second = jax.nn.relu(normed_two).astype(jnp.bfloat16)
    expanded = map_product(second, expand_w)
    mean_three, var_three, normed_three = batch_norm(
        expanded, gain_now[2 * middle :], bias_now[2 * middle :], row_count
    )
    block_out = jax.nn.relu(normed_three + activations.astype(jnp.float32))
    pooled = jnp.mean(block_out, axis=(1, 2)).astype(jnp.bfloat16)
    logits = (
        lax.dot_general(
            pooled, class_w, (((1,), (1,)), ((), ())), preferred_element_type=jnp.float32
        )
        + shift_now
    )
    classes = logits.shape[1]
    onehot = labels[:, None] == jnp.arange(classes, dtype=jnp.int32)[None, :]
    correct = jnp.sum(jnp.where(onehot, logits, 0.0), axis=1)
    rivals = jnp.max(jnp.where(onehot, -1e30, logits), axis=1)
    partial_value = jnp.sum(correct - rivals) / (images * lax.axis_size("batch"))
    point_count = point_index.shape[0]
    placed = jnp.where(
        jnp.arange(point_count, dtype=jnp.int32) == lax.axis_index("point"), partial_value, 0.0
    )
    margin_all = lax.psum(placed, ("point", "batch"))
    return (
        mean_one[None],
        var_one[None],
        mean_two[None],
        var_two[None],
        mean_three[None],
        var_three[None],
        margin_all,
    )


def solution(mesh):
    placed = (
        P("batch", None, None, None),
        P("batch"),
        P(),
        P(),
        P(None, "point", None),
        P(None, "point", None),
        P(None, "point", None),
        P(None, None, "point"),
        P(),
        P(),
        P(),
    )
    return jax.shard_map(
        shards,
        mesh=mesh,
        in_specs=placed,
        out_specs=(
            P("point", None),
            P("point", None),
            P("point", None),
            P("point", None),
            P("point", None),
            P("point", None),
            P(),
        ),
        check_vma=False,
    )
```

profile of v0, /device:TPU:0, one launch (start us, length us, event | category | flops | bytes accessed | tf_op | source)
XLA Modules:
  0.0 208.5 jit_solution(10090536275269189656)
XLA Ops:
  7.2 0.0 all-gather.5.cloned.1.call-start
  7.2 0.7 all-gather.5.cloned.1.call-update
  7.9 0.0 all-gather.7.cloned.1.call-start
  7.9 0.7 all-gather.7.cloned.1.call-update
  8.7 0.0 all-gather.9.cloned.1.call-start
  8.7 0.7 all-gather.9.cloned.1.call-update
  9.4 0.0 all-gather.11.cloned.1.call-start
  9.4 0.5 all-gather.11.cloned.1.call-update
  10.0 0.9 select_reduce_fusion.2
  10.8 0.1 constant_dynamic-slice_fusion
  10.9 0.6 fusion.37
  11.5 2.8 %multiply_add_fusion = (f32[1,1536]{1,0:T(1,128)S(1)}, f32[1,1536]{1,0:T(1,128)S(1)}) fusion(f32[3,1536]{1,0:T(4,128)} %param.20, f32[]{:T(128)} %bitcast.5, f32[]{:T(128)} %bitcast.4, f32[]{:T(128)} %bitcast.3, f32[3,1536]{1,0:T(4,128)} %param.19), kind=kLoop, calls=%fused_computation.50 | loop fusion | flops 15360 | bytes 49164 | tf_op jit(solution)/shard_map/add | solution.py:29
  14.3 2.7 %multiply_add_fusion.2 = f32[1,1000]{1,0:T(1,128)S(1)} fusion(f32[3,1000]{1,0:T(4,128)} %param.21, f32[]{:T(128)} %bitcast.5, f32[]{:T(128)} %bitcast.4, f32[]{:T(128)} %bitcast.3), kind=kLoop, calls=%fused_computation.52 | loop fusion | flops 5000 | bytes 16012 | tf_op jit(solution)/shard_map/add | solution.py:29
  17.0 21.2 %all-gather.5.cloned.1.call-done = bf16[3,1024,256]{2,1,0:T(8,128)(2,1)} async-done(((bf16[3,128,256]{2,1,0:T(8,128)(2,1)}), bf16[3,1024,256]{2,1,0:T(8,128)(2,1)}) %all-gather.5.cloned.1.call-update) | async-done | bytes 1572880 | tf_op jit(solution)/shard_map/all_gather | solution.py:36
  38.2 13.3 %multiply_reduce_fusion.2 = (f32[256]{0:T(256)S(1)}, f32[256]{0:T(256)S(1)}, f32[256,32,14,14]{0,1,3,2:T(8,128)}) fusion(bf16[32,14,14,1024]{3,0,2,1:T(8,128)(2,1)} %param.11, bf16[3,1024,256]{2,1,0:T(8,128)(2,1)} %all-gather.5.cloned.1.call-done, f32[]{:T(128)} %bitcast.5, f32[]{:T(128)} %bitcast.4, f32[]{:T(128)} %bitcast.3), kind=kOutput, calls=%fused_computation.7 | convolution fusion | flops 3295510016 | bytes 20842508 | tf_op jit(solution)/shard_map/dot_general | solution.py:41
  51.5 11.7 %all-reduce.3 = (f32[256]{0:T(256)S(1)}, f32[256]{0:T(256)S(1)}) all-reduce(f32[256]{0:T(256)S(1)} %get-tuple-element.12, f32[256]{0:T(256)S(1)} %get-tuple-element.11), channel_id=1, replica_groups=mesh['point'=8,'batch'=4] {'batch'}, use_global_device_ids=true, to_apply=%region_2.3 | all-reduce | flops 512 | bytes 4096 | tf_op jit(solution)/shard_map/psum | solution.py:47
  63.2 0.6 add_rsqrt_fusion.2
  63.8 0.0 copy-start.4
  63.8 4.1 %fusion.1 = bf16[32,14,14,256]{3,0,2,1:T(8,128)(2,1)S(1)} fusion(f32[256,32,14,14]{0,1,3,2:T(8,128)} %get-tuple-element.43, f32[256]{0:T(256)S(1)} %bitcast.77, f32[256]{0:T(256)S(1)} %bitcast.78, f32[256]{0:T(256)S(1)} %get-tuple-element.25, f32[256]{0:T(256)S(1)} %get-tuple-element.39), kind=kLoop, calls=%fused_computation.13 | loop fusion | flops 9633792 | bytes 9637888 | tf_op jit(solution)/shard_map/convert_element_type | solution.py:103
  67.9 4.9 %pad_slice_fusion.2 = (bf16[32,16,14,256]{3,0,2,1:T(8,128)(2,1)}, bf16[32,16,14,256]{3,0,2,1:T(8,128)(2,1)}, bf16[32,16,14,256]{3,0,2,1:T(8,128)(2,1)}) fusion(bf16[32,14,14,256]{3,0,2,1:T(8,128)(2,1)S(1)} %fusion.1), kind=kLoop, calls=%fused_computation.10 | loop fusion | bytes 14221312 | tf_op jit(solution)/shard_map/slice | solution.py:62
  72.8 0.0 copy-done.4
  72.8 1.2 all-gather.7.cloned.1.call-done
  74.0 4.5 %add_convert_fusion.1 = bf16[1,2304,256]{2,1,0:T(8,128)(2,1)S(1)} fusion(bf16[3,2304,256]{2,1,0:T(8,128)(2,1)} %all-gather.7.cloned.1.call-done, f32[]{:T(128)} %bitcast.5, f32[]{:T(128)} %bitcast.4, f32[]{:T(128)} %bitcast.3), kind=kLoop, calls=%fused_computation.19 | loop fusion | flops 5308416 | bytes 4718604 | tf_op jit(solution)/shard_map/convert_element_type | solution.py:37
  78.5 0.0 copy-start
  78.5 0.0 copy-start.1
  78.5 0.0 copy-start.2
  78.5 7.3 %fusion.31 = f32[32,14,14,256]{3,0,2,1:T(8,128)} fusion(bf16[1,2304,256]{2,1,0:T(8,128)(2,1)S(1)} %add_convert_fusion.1, bf16[32,16,14,256]{3,0,2,1:T(8,128)(2,1)} %get-tuple-element.29, bf16[32,16,14,256]{3,0,2,1:T(8,128)(2,1)} %get-tuple-element.28, bf16[32,16,14,256]{3,0,2,1:T(8,128)(2,1)} %get-tuple-element.27), kind=kOutput, calls=%fused_computation.44 | convolution fusion | flops 2499280896 | bytes 17825792 | tf_op jit(solution)/shard_map/dot_general | solution.py:41
  85.8 0.0 copy-done
  85.8 1.2 copy-done.1
  87.0 1.0 copy-done.2
  88.0 5.4 %fusion.30 = f32[32,14,14,256]{3,0,2,1:T(8,128)} fusion(bf16[1,2304,256]{2,1,0:T(8,128)(2,1)S(1)} %add_convert_fusion.1, bf16[32,16,14,256]{3,0,2,1:T(8,128)(2,1)S(1)} %copy-done.2, bf16[32,16,14,256]{3,0,2,1:T(8,128)(2,1)S(1)} %copy-done.1, bf16[32,16,14,256]{3,0,2,1:T(8,128)(2,1)S(1)} %copy-done), kind=kOutput, calls=%fused_computation.42 | convolution fusion | flops 2499280896 | bytes 17825792 | tf_op jit(solution)/shard_map/dot_general | solution.py:41
  93.4 9.0 %multiply_reduce_fusion.1 = (f32[256]{0:T(256)S(1)}, f32[256]{0:T(256)S(1)}, f32[32,14,14,256]{3,0,2,1:T(8,128)}) fusion(bf16[1,2304,256]{2,1,0:T(8,128)(2,1)S(1)} %add_convert_fusion.1, bf16[32,16,14,256]{3,0,2,1:T(8,128)(2,1)S(1)} %copy-done.2, bf16[32,16,14,256]{3,0,2,1:T(8,128)(2,1)S(1)} %copy-done.1, bf16[32,16,14,256]{3,0,2,1:T(8,128)(2,1)S(1)} %copy-done, ...), kind=kOutput, calls=%fused_computation.5 | convolution fusion | flops 2507308544 | bytes 30672896 | tf_op jit(solution)/shard_map/dot_general | solution.py:41
  102.4 11.9 %all-reduce.2 = (f32[256]{0:T(256)S(1)}, f32[256]{0:T(256)S(1)}) all-reduce(f32[256]{0:T(256)S(1)} %get-tuple-element.10, f32[256]{0:T(256)S(1)} %get-tuple-element.9), channel_id=1, replica_groups=mesh['point'=8,'batch'=4] {'batch'}, use_global_device_ids=true, to_apply=%region_6.7 | all-reduce | flops 512 | bytes 4096 | tf_op jit(solution)/shard_map/psum | solution.py:47
  114.4 0.6 add_rsqrt_fusion.1
  114.9 0.0 copy-start.5
  114.9 0.0 all-gather.9.cloned.1.call-done
  114.9 16.0 %multiply_reduce_fusion = (f32[1024]{0:T(1024)S(1)}, f32[1024]{0:T(1024)S(1)}, f32[32,14,14,1024]{3,0,2,1:T(8,128)}) fusion(bf16[3,256,1024]{2,1,0:T(8,128)(2,1)} %all-gather.9.cloned.1.call-done, f32[]{:T(128)} %bitcast.5, f32[]{:T(128)} %bitcast.4, f32[]{:T(128)} %bitcast.3, f32[32,14,14,256]{3,0,2,1:T(8,128)} %get-tuple-element.44, f32[256]{0:T(256)S(1)} %bitcast.84, ...), kind=kOutput, calls=%fused_computation.1 | convolution fusion | flops 3319592960 | bytes 33697804 | tf_op jit(solution)/shard_map/dot_general | solution.py:41
  130.9 0.0 copy-done.5
  130.9 8.5 %all-reduce.1 = (f32[1024]{0:T(1024)S(1)}, f32[1024]{0:T(1024)S(1)}) all-reduce(f32[1024]{0:T(1024)S(1)} %get-tuple-element.8, f32[1024]{0:T(1024)S(1)} %get-tuple-element.7), channel_id=1, replica_groups=mesh['point'=8,'batch'=4] {'batch'}, use_global_device_ids=true, to_apply=%region_10.11 | all-reduce | flops 2048 | bytes 16384 | tf_op jit(solution)/shard_map/psum | solution.py:47
  139.5 0.6 add_rsqrt_fusion
  140.1 0.0 copy-start.3
  140.1 0.0 copy-start.6
  140.1 14.9 %maximum_reduce_fusion = f32[32,1024]{1,0:T(8,128)S(1)} fusion(bf16[32,14,14,1024]{3,0,2,1:T(8,128)(2,1)} %param.11, f32[32,14,14,1024]{3,0,2,1:T(8,128)} %get-tuple-element.45, f32[1024]{0:T(1024)S(1)} %bitcast.74, f32[1024]{0:T(1024)S(1)} %bitcast.75, f32[1024]{0:T(1024)S(1)} %get-tuple-element.21, f32[1024]{0:T(1024)S(1)} %get-tuple-element.34), kind=kLoop, calls=%fused_computation | loop fusion | flops 51347456 | bytes 38682624 | tf_op jit(solution)/shard_map/reduce_sum | solution.py:114
  154.9 0.0 copy-done.3
  154.9 0.0 all-gather.11.cloned.1.call-done
  155.0 0.0 copy-done.6
  155.0 6.1 %select_reduce_fusion = (f32[32]{0:T(128)S(1)}, f32[32]{0:T(128)S(1)}) fusion(s32[32]{0:T(128)S(1)} %copy-done.6, f32[1000]{0:T(1024)S(1)} %bitcast.80, bf16[3,1000,1024]{2,1,0:T(8,128)(2,1)} %all-gather.11.cloned.1.call-done, f32[]{:T(128)} %bitcast.5, f32[]{:T(128)} %bitcast.4, f32[]{:T(128)} %bitcast.3, f32[32,1024]{1,0:T(8,128)S(1)} %maximum_reduce_fusion), kind=kOutput, calls=%fused_computation.45 | convolution fusion | flops 75009472 | bytes 6279468 | tf_op jit(solution)/shard_map/dot_general | solution.py:116
  161.1 0.6 subtract_reduce_fusion
  162.4 39.6 %psum.55 = f32[8]{0:T(128)} all-reduce(f32[8]{0:T(128)S(1)} %compare_select_fusion), channel_id=1, replica_groups=mesh['point'=8,'batch'=4] {'point','batch'}, use_global_device_ids=true, to_apply=%region_17.18 | all-reduce | flops 8 | bytes 64 | tf_op jit(solution)/shard_map/psum | solution.py:130
  (7 shorter events, 0.0 us)
Async XLA Ops:
  7.2 31.0 %all-gather.5.cloned.1.call-start = ((), (), s32[]{:S(2)}) async-start(), calls=%async_computation | async-start | bytes 1769472 | tf_op jit(solution)/shard_map/all_gather | solution.py:36
  7.9 66.1 %all-gather.7.cloned.1.call-start = ((), (), s32[]{:S(2)}) async-start(), calls=%async_computation.1 | async-start | bytes 3981312 | tf_op jit(solution)/shard_map/all_gather | solution.py:36
  8.7 106.3 %all-gather.9.cloned.1.call-start = ((), (), s32[]{:S(2)}) async-start(), calls=%async_computation.2 | async-start | bytes 1769472 | tf_op jit(solution)/shard_map/all_gather | solution.py:36
  9.4 145.6 %all-gather.11.cloned.1.call-start = ((), (), s32[]{:S(2)}) async-start(), calls=%async_computation.3 | async-start | bytes 6912000 | tf_op jit(solution)/shard_map/all_gather | solution.py:34
  63.8 9.0 %copy-start.4 = (f32[256]{0:T(256)}, f32[256]{0:T(256)S(1)}, u32[]{:S(2)}) copy-start(f32[256]{0:T(256)S(1)} %get-tuple-element.39) | copy-start | bytes 3076
  78.5 7.3 %copy-start = (bf16[32,16,14,256]{3,0,2,1:T(8,128)(2,1)S(1)}, bf16[32,16,14,256]{3,0,2,1:T(8,128)(2,1)}, u32[]{:S(2)}) copy-start(bf16[32,16,14,256]{3,0,2,1:T(8,128)(2,1)} %get-tuple-element.27) | copy-start | bytes 11010052
  78.5 8.5 %copy-start.1 = (bf16[32,16,14,256]{3,0,2,1:T(8,128)(2,1)S(1)}, bf16[32,16,14,256]{3,0,2,1:T(8,128)(2,1)}, u32[]{:S(2)}) copy-start(bf16[32,16,14,256]{3,0,2,1:T(8,128)(2,1)} %get-tuple-element.28) | copy-start | bytes 11010052
  78.5 9.5 %copy-start.2 = (bf16[32,16,14,256]{3,0,2,1:T(8,128)(2,1)S(1)}, bf16[32,16,14,256]{3,0,2,1:T(8,128)(2,1)}, u32[]{:S(2)}) copy-start(bf16[32,16,14,256]{3,0,2,1:T(8,128)(2,1)} %get-tuple-element.29) | copy-start | bytes 11010052
  114.9 16.0 %copy-start.5 = (f32[256]{0:T(256)}, f32[256]{0:T(256)S(1)}, u32[]{:S(2)}) copy-start(f32[256]{0:T(256)S(1)} %get-tuple-element.38) | copy-start | bytes 3076
  140.1 14.9 %copy-start.3 = (f32[1024]{0:T(1024)}, f32[1024]{0:T(1024)S(1)}, u32[]{:S(2)}) copy-start(f32[1024]{0:T(1024)S(1)} %get-tuple-element.34) | copy-start | bytes 12292
  140.1 14.9 %copy-start.6 = (s32[32]{0:T(128)S(1)}, s32[32]{0:T(128)}, u32[]{:S(2)}) copy-start(s32[32]{0:T(128)} %param.12) | copy-start | bytes 388
Sparse Core Ops, SparseCore 0:
  9.9 28.2 all-gather.4
  40.1 33.8 all-gather.6
  75.9 25.5 all-gather.8
  103.2 45.9 all-gather.10
where the time goes:
time: 209 us; the launch traced here: 208 us
  blocking collectives  71.7 us (34%)
  matrix products  57.1 us (27%)
  other arithmetic  32.2 us (15%)
  waiting for transfers between devices  24.9 us (12%)
  between operations  14.6 us (7%)
  local copies, waits for them, and re-layouts  7.82 us (4%)
    dot_general x5, matrix products, map_product(): lax.dot_general(maps, kernel, (((3,), (0,)), ((), ())), preferred_element...  51 us
    psum x1, blocking collectives, shards(): margin_all = lax.psum(placed, ('point', 'batch'))  39.6 us
    psum x3, blocking collectives, batch_norm(): lax.psum((jnp.sum(pre_norm, axis=(0, 1, 2)), jnp.sum(pre_norm * pre_norm,...  32.1 us
    all_gather x3, waiting for transfers between devices, point_weight(): gathered = lax.all_gather(endpoints, 'point', axis=1, tiled=True)  22.3 us
    reduce_sum x1, other arithmetic, shards(): pooled = jnp.mean(block_out, axis=(1, 2)).astype(jnp.bfloat16)  14.9 us
    dot_general x1, matrix products, shards(): lax.dot_general(pooled, class_w, (((1,), (1,)), ((), ())), preferred_elem...  6.09 us
    add x2, other arithmetic, blend_all(): return start_part + bend_part + final_part  5.52 us
    slice x1, local copies, waits for them, and re-layouts, spatial_conv(): padded[:, :, 0:side_len, :]  4.94 us
  transfers between devices with their start and end apart: 4, of which 2 were waited for; matrix products, arithmetic and copies ran while one was open for 42% of the time, Pallas kernels for 0%

commit v1 on v0

--- a/solution.py
+++ b/solution.py
@@ -4,6 +4,12 @@
 from jax.sharding import PartitionSpec as P
 
 EPSILON = 1e-05
+
+
+def summed_here(block, mesh_axis):
+    parts = lax.all_gather(block, mesh_axis, axis=0, tiled=False)
+    acc = parts.sum(axis=0)
+    return acc
 
 
 def curve_coefficients(t_values, point_index):
@@ -127,7 +133,7 @@
     placed = jnp.where(
         jnp.arange(point_count, dtype=jnp.int32) == lax.axis_index("point"), partial_value, 0.0
     )
-    margin_all = lax.psum(placed, ("point", "batch"))
+    margin_all = summed_here(placed, ("point", "batch"))
     return (
         mean_one[None],
         var_one[None],

time: 209 us -> 235 us (1.12)
  blocking collectives: 71.7 us -> 97.4 us
    all_gather x0 -> x1, blocking collectives: none -> 65.3 us  [summed_here(): parts = lax.all_gather(block, mesh_axis, axis=0, tiled=False)]
    psum x1 -> x0, blocking collectives: 39.6 us -> none  [shards(): margin_all = lax.psum(placed, ('point', 'batch'))]
  transfers between devices with their start and end apart: 4 -> 4, of which waited for: 2 -> 2; matrix products, arithmetic and copies ran while one was open for 42% -> 38% of each run, Pallas kernels for 0% -> 0%
where the time goes in v1:
time: 235 us
  blocking collectives  97.4 us (41%)
  matrix products  57.1 us (24%)
  other arithmetic  32.8 us (14%)
  waiting for transfers between devices  24.9 us (11%)
  between operations  14.6 us (6%)
  local copies, waits for them, and re-layouts  7.82 us (3%)
    all_gather x1, blocking collectives, summed_here(): parts = lax.all_gather(block, mesh_axis, axis=0, tiled=False)  65.3 us
    dot_general x5, matrix products, map_product(): lax.dot_general(maps, kernel, (((3,), (0,)), ((), ())), preferred_element...  51 us
    psum x3, blocking collectives, batch_norm(): lax.psum((jnp.sum(pre_norm, axis=(0, 1, 2)), jnp.sum(pre_norm * pre_norm,...  32.1 us
    all_gather x3, waiting for transfers between devices, point_weight(): gathered = lax.all_gather(endpoints, 'point', axis=1, tiled=True)  22.3 us
    reduce_sum x1, other arithmetic, shards(): pooled = jnp.mean(block_out, axis=(1, 2)).astype(jnp.bfloat16)  14.9 us
    dot_general x1, matrix products, shards(): lax.dot_general(pooled, class_w, (((1,), (1,)), ((), ())), preferred_elem...  6.09 us
    add x2, other arithmetic, blend_all(): return start_part + bend_part + final_part  5.52 us
    slice x1, local copies, waits for them, and re-layouts, spatial_conv(): padded[:, :, 0:side_len, :]  4.94 us
  transfers between devices with their start and end apart: 4, of which 2 were waited for; matrix products, arithmetic and copies ran while one was open for 38% of the time, Pallas kernels for 0%

profile of v1, /device:TPU:0, one launch (start us, length us, event | category | flops | bytes accessed | tf_op | source)
XLA Modules:
  0.0 234.8 jit_solution(11276874742730836106)
XLA Ops:
  7.2 0.0 all-gather.6.cloned.1.call-start
  7.2 0.7 all-gather.6.cloned.1.call-update
  7.9 0.0 all-gather.8.cloned.1.call-start
  7.9 0.7 all-gather.8.cloned.1.call-update
  8.7 0.0 all-gather.10.cloned.1.call-start
  8.7 0.7 all-gather.10.cloned.1.call-update
  9.4 0.0 all-gather.12.cloned.1.call-start
  9.4 0.5 all-gather.12.cloned.1.call-update
  10.0 0.9 select_reduce_fusion.2
  10.8 0.1 constant_dynamic-slice_fusion
  10.9 0.6 fusion.38
  11.5 2.8 %multiply_add_fusion = (f32[1,1536]{1,0:T(1,128)S(1)}, f32[1,1536]{1,0:T(1,128)S(1)}) fusion(f32[3,1536]{1,0:T(4,128)} %param.20, f32[]{:T(128)} %bitcast.5, f32[]{:T(128)} %bitcast.4, f32[]{:T(128)} %bitcast.3, f32[3,1536]{1,0:T(4,128)} %param.19), kind=kLoop, calls=%fused_computation.50 | loop fusion | flops 15360 | bytes 49164 | tf_op jit(solution)/shard_map/add | solution.py:35
  14.3 2.7 %multiply_add_fusion.2 = f32[1,1000]{1,0:T(1,128)S(1)} fusion(f32[3,1000]{1,0:T(4,128)} %param.21, f32[]{:T(128)} %bitcast.5, f32[]{:T(128)} %bitcast.4, f32[]{:T(128)} %bitcast.3), kind=kLoop, calls=%fused_computation.52 | loop fusion | flops 5000 | bytes 16012 | tf_op jit(solution)/shard_map/add | solution.py:35
  17.0 21.2 %all-gather.6.cloned.1.call-done = bf16[3,1024,256]{2,1,0:T(8,128)(2,1)} async-done(((bf16[3,128,256]{2,1,0:T(8,128)(2,1)}), bf16[3,1024,256]{2,1,0:T(8,128)(2,1)}) %all-gather.6.cloned.1.call-update) | async-done | bytes 1572880 | tf_op jit(solution)/shard_map/all_gather | solution.py:42
  38.2 13.3 %multiply_reduce_fusion.2 = (f32[256]{0:T(256)S(1)}, f32[256]{0:T(256)S(1)}, f32[256,32,14,14]{0,1,3,2:T(8,128)}) fusion(bf16[32,14,14,1024]{3,0,2,1:T(8,128)(2,1)} %param.11, bf16[3,1024,256]{2,1,0:T(8,128)(2,1)} %all-gather.6.cloned.1.call-done, f32[]{:T(128)} %bitcast.5, f32[]{:T(128)} %bitcast.4, f32[]{:T(128)} %bitcast.3), kind=kOutput, calls=%fused_computation.7 | convolution fusion | flops 3295510016 | bytes 20842508 | tf_op jit(solution)/shard_map/dot_general | solution.py:47
  51.5 11.7 %all-reduce.3 = (f32[256]{0:T(256)S(1)}, f32[256]{0:T(256)S(1)}) all-reduce(f32[256]{0:T(256)S(1)} %get-tuple-element.12, f32[256]{0:T(256)S(1)} %get-tuple-element.11), channel_id=1, replica_groups=mesh['point'=8,'batch'=4] {'batch'}, use_global_device_ids=true, to_apply=%region_2.3 | all-reduce | flops 512 | bytes 4096 | tf_op jit(solution)/shard_map/psum | solution.py:53
  63.2 0.6 add_rsqrt_fusion.2
  63.8 0.0 copy-start.4
  63.8 4.1 %fusion.1 = bf16[32,14,14,256]{3,0,2,1:T(8,128)(2,1)S(1)} fusion(f32[256,32,14,14]{0,1,3,2:T(8,128)} %get-tuple-element.43, f32[256]{0:T(256)S(1)} %bitcast.79, f32[256]{0:T(256)S(1)} %bitcast.80, f32[256]{0:T(256)S(1)} %get-tuple-element.25, f32[256]{0:T(256)S(1)} %get-tuple-element.39), kind=kLoop, calls=%fused_computation.13 | loop fusion | flops 9633792 | bytes 9637888 | tf_op jit(solution)/shard_map/convert_element_type | solution.py:109
  67.9 4.9 %pad_slice_fusion.2 = (bf16[32,16,14,256]{3,0,2,1:T(8,128)(2,1)}, bf16[32,16,14,256]{3,0,2,1:T(8,128)(2,1)}, bf16[32,16,14,256]{3,0,2,1:T(8,128)(2,1)}) fusion(bf16[32,14,14,256]{3,0,2,1:T(8,128)(2,1)S(1)} %fusion.1), kind=kLoop, calls=%fused_computation.10 | loop fusion | bytes 14221312 | tf_op jit(solution)/shard_map/slice | solution.py:68
  72.8 0.0 copy-done.4
  72.8 1.2 all-gather.8.cloned.1.call-done
  74.0 4.5 %add_convert_fusion.1 = bf16[1,2304,256]{2,1,0:T(8,128)(2,1)S(1)} fusion(bf16[3,2304,256]{2,1,0:T(8,128)(2,1)} %all-gather.8.cloned.1.call-done, f32[]{:T(128)} %bitcast.5, f32[]{:T(128)} %bitcast.4, f32[]{:T(128)} %bitcast.3), kind=kLoop, calls=%fused_computation.19 | loop fusion | flops 5308416 | bytes 4718604 | tf_op jit(solution)/shard_map/convert_element_type | solution.py:43
  78.5 0.0 copy-start
  78.5 0.0 copy-start.1
  78.5 0.0 copy-start.2
  78.5 7.3 %fusion.31 = f32[32,14,14,256]{3,0,2,1:T(8,128)} fusion(bf16[1,2304,256]{2,1,0:T(8,128)(2,1)S(1)} %add_convert_fusion.1, bf16[32,16,14,256]{3,0,2,1:T(8,128)(2,1)} %get-tuple-element.29, bf16[32,16,14,256]{3,0,2,1:T(8,128)(2,1)} %get-tuple-element.28, bf16[32,16,14,256]{3,0,2,1:T(8,128)(2,1)} %get-tuple-element.27), kind=kOutput, calls=%fused_computation.44 | convolution fusion | flops 2499280896 | bytes 17825792 | tf_op jit(solution)/shard_map/dot_general | solution.py:47
  85.8 0.0 copy-done
  85.8 1.2 copy-done.1
  87.0 1.0 copy-done.2
  88.0 5.4 %fusion.30 = f32[32,14,14,256]{3,0,2,1:T(8,128)} fusion(bf16[1,2304,256]{2,1,0:T(8,128)(2,1)S(1)} %add_convert_fusion.1, bf16[32,16,14,256]{3,0,2,1:T(8,128)(2,1)S(1)} %copy-done.2, bf16[32,16,14,256]{3,0,2,1:T(8,128)(2,1)S(1)} %copy-done.1, bf16[32,16,14,256]{3,0,2,1:T(8,128)(2,1)S(1)} %copy-done), kind=kOutput, calls=%fused_computation.42 | convolution fusion | flops 2499280896 | bytes 17825792 | tf_op jit(solution)/shard_map/dot_general | solution.py:47
  93.4 9.0 %multiply_reduce_fusion.1 = (f32[256]{0:T(256)S(1)}, f32[256]{0:T(256)S(1)}, f32[32,14,14,256]{3,0,2,1:T(8,128)}) fusion(bf16[1,2304,256]{2,1,0:T(8,128)(2,1)S(1)} %add_convert_fusion.1, bf16[32,16,14,256]{3,0,2,1:T(8,128)(2,1)S(1)} %copy-done.2, bf16[32,16,14,256]{3,0,2,1:T(8,128)(2,1)S(1)} %copy-done.1, bf16[32,16,14,256]{3,0,2,1:T(8,128)(2,1)S(1)} %copy-done, ...), kind=kOutput, calls=%fused_computation.5 | convolution fusion | flops 2507308544 | bytes 30672896 | tf_op jit(solution)/shard_map/dot_general | solution.py:47
  102.4 11.9 %all-reduce.2 = (f32[256]{0:T(256)S(1)}, f32[256]{0:T(256)S(1)}) all-reduce(f32[256]{0:T(256)S(1)} %get-tuple-element.10, f32[256]{0:T(256)S(1)} %get-tuple-element.9), channel_id=1, replica_groups=mesh['point'=8,'batch'=4] {'batch'}, use_global_device_ids=true, to_apply=%region_6.7 | all-reduce | flops 512 | bytes 4096 | tf_op jit(solution)/shard_map/psum | solution.py:53
  114.4 0.6 add_rsqrt_fusion.1
  114.9 0.0 copy-start.5
  114.9 0.0 all-gather.10.cloned.1.call-done
  114.9 16.0 %multiply_reduce_fusion = (f32[1024]{0:T(1024)S(1)}, f32[1024]{0:T(1024)S(1)}, f32[32,14,14,1024]{3,0,2,1:T(8,128)}) fusion(bf16[3,256,1024]{2,1,0:T(8,128)(2,1)} %all-gather.10.cloned.1.call-done, f32[]{:T(128)} %bitcast.5, f32[]{:T(128)} %bitcast.4, f32[]{:T(128)} %bitcast.3, f32[32,14,14,256]{3,0,2,1:T(8,128)} %get-tuple-element.44, f32[256]{0:T(256)S(1)} %bitcast.86, ...), kind=kOutput, calls=%fused_computation.1 | convolution fusion | flops 3319592960 | bytes 33697804 | tf_op jit(solution)/shard_map/dot_general | solution.py:47
  130.9 0.0 copy-done.5
  130.9 8.5 %all-reduce.1 = (f32[1024]{0:T(1024)S(1)}, f32[1024]{0:T(1024)S(1)}) all-reduce(f32[1024]{0:T(1024)S(1)} %get-tuple-element.8, f32[1024]{0:T(1024)S(1)} %get-tuple-element.7), channel_id=1, replica_groups=mesh['point'=8,'batch'=4] {'batch'}, use_global_device_ids=true, to_apply=%region_10.11 | all-reduce | flops 2048 | bytes 16384 | tf_op jit(solution)/shard_map/psum | solution.py:53
  139.5 0.6 add_rsqrt_fusion
  140.1 0.0 copy-start.3
  140.1 0.0 copy-start.6
  140.1 14.9 %maximum_reduce_fusion = f32[32,1024]{1,0:T(8,128)S(1)} fusion(bf16[32,14,14,1024]{3,0,2,1:T(8,128)(2,1)} %param.11, f32[32,14,14,1024]{3,0,2,1:T(8,128)} %get-tuple-element.45, f32[1024]{0:T(1024)S(1)} %bitcast.76, f32[1024]{0:T(1024)S(1)} %bitcast.77, f32[1024]{0:T(1024)S(1)} %get-tuple-element.21, f32[1024]{0:T(1024)S(1)} %get-tuple-element.34), kind=kLoop, calls=%fused_computation | loop fusion | flops 51347456 | bytes 38682624 | tf_op jit(solution)/shard_map/reduce_sum | solution.py:120
  154.9 0.0 copy-done.3
  154.9 0.0 all-gather.12.cloned.1.call-done
  155.0 0.0 copy-done.6
  155.0 6.1 %select_reduce_fusion = (f32[32]{0:T(128)S(1)}, f32[32]{0:T(128)S(1)}) fusion(s32[32]{0:T(128)S(1)} %copy-done.6, f32[1000]{0:T(1024)S(1)} %bitcast.82, bf16[3,1000,1024]{2,1,0:T(8,128)(2,1)} %all-gather.12.cloned.1.call-done, f32[]{:T(128)} %bitcast.5, f32[]{:T(128)} %bitcast.4, f32[]{:T(128)} %bitcast.3, f32[32,1024]{1,0:T(8,128)S(1)} %maximum_reduce_fusion), kind=kOutput, calls=%fused_computation.45 | convolution fusion | flops 75009472 | bytes 6279468 | tf_op jit(solution)/shard_map/dot_general | solution.py:122
  161.1 0.6 subtract_reduce_fusion
  162.4 65.3 %all-gather = f32[32,1,8]{2,1,0:T(1,128)S(1)} all-gather(f32[1,1,8]{2,1,0:T(1,128)S(1)} %fusion.33), channel_id=1, replica_groups=mesh['point'=8,'batch'=4] {'point','batch'}, dimensions={0}, use_global_device_ids=true | all-gather | bytes 1056 | tf_op jit(solution)/shard_map/all_gather | solution.py:10
  227.7 0.6 reduce_sum.109
  (7 shorter events, 0.0 us)
Async XLA Ops:
  7.2 31.0 %all-gather.6.cloned.1.call-start = ((), (), s32[]{:S(2)}) async-start(), calls=%async_computation | async-start | bytes 1769472 | tf_op jit(solution)/shard_map/all_gather | solution.py:42
  7.9 66.1 %all-gather.8.cloned.1.call-start = ((), (), s32[]{:S(2)}) async-start(), calls=%async_computation.1 | async-start | bytes 3981312 | tf_op jit(solution)/shard_map/all_gather | solution.py:42
  8.7 106.3 %all-gather.10.cloned.1.call-start = ((), (), s32[]{:S(2)}) async-start(), calls=%async_computation.2 | async-start | bytes 1769472 | tf_op jit(solution)/shard_map/all_gather | solution.py:42
  9.4 145.6 %all-gather.12.cloned.1.call-start = ((), (), s32[]{:S(2)}) async-start(), calls=%async_computation.3 | async-start | bytes 6912000 | tf_op jit(solution)/shard_map/all_gather | solution.py:40
  63.8 9.0 %copy-start.4 = (f32[256]{0:T(256)}, f32[256]{0:T(256)S(1)}, u32[]{:S(2)}) copy-start(f32[256]{0:T(256)S(1)} %get-tuple-element.39) | copy-start | bytes 3076
  78.5 7.3 %copy-start = (bf16[32,16,14,256]{3,0,2,1:T(8,128)(2,1)S(1)}, bf16[32,16,14,256]{3,0,2,1:T(8,128)(2,1)}, u32[]{:S(2)}) copy-start(bf16[32,16,14,256]{3,0,2,1:T(8,128)(2,1)} %get-tuple-element.27) | copy-start | bytes 11010052
  78.5 8.5 %copy-start.1 = (bf16[32,16,14,256]{3,0,2,1:T(8,128)(2,1)S(1)}, bf16[32,16,14,256]{3,0,2,1:T(8,128)(2,1)}, u32[]{:S(2)}) copy-start(bf16[32,16,14,256]{3,0,2,1:T(8,128)(2,1)} %get-tuple-element.28) | copy-start | bytes 11010052
  78.5 9.5 %copy-start.2 = (bf16[32,16,14,256]{3,0,2,1:T(8,128)(2,1)S(1)}, bf16[32,16,14,256]{3,0,2,1:T(8,128)(2,1)}, u32[]{:S(2)}) copy-start(bf16[32,16,14,256]{3,0,2,1:T(8,128)(2,1)} %get-tuple-element.29) | copy-start | bytes 11010052
  114.9 16.0 %copy-start.5 = (f32[256]{0:T(256)}, f32[256]{0:T(256)S(1)}, u32[]{:S(2)}) copy-start(f32[256]{0:T(256)S(1)} %get-tuple-element.38) | copy-start | bytes 3076
  140.1 14.9 %copy-start.3 = (f32[1024]{0:T(1024)}, f32[1024]{0:T(1024)S(1)}, u32[]{:S(2)}) copy-start(f32[1024]{0:T(1024)S(1)} %get-tuple-element.34) | copy-start | bytes 12292
  140.1 14.9 %copy-start.6 = (s32[32]{0:T(128)S(1)}, s32[32]{0:T(128)}, u32[]{:S(2)}) copy-start(s32[32]{0:T(128)} %param.12) | copy-start | bytes 388
Sparse Core Ops, SparseCore 0:
  9.9 28.2 all-gather.5
  40.1 33.8 all-gather.7
  75.9 25.5 all-gather.9
  103.2 45.9 all-gather.11
